TPU v7x, 32 devices: a whole 2x2x4 slice. The times are simulated.
32 devices in a mesh: seq: 8 (over z, x), hid: 4 (over y, core).
Axes of the slice: x: 2, y: 2, z: 4, core: 2. Of those that a mesh axis runs over, the one named last changes fastest.
Arguments:
- tokens: bfloat16 [1024, 4096], P('seq', 'hid'), may hold values from -6 to 6
- hidden_grad: bfloat16 [1024, 14336], P('seq', 'hid'), may hold values from -6 to 6
- gate_blocks: bfloat16 [4, 448, 128, 128], P('hid', 'seq'), may hold values from -0.125 to 0.125
- up_blocks: bfloat16 [4, 448, 128, 128], P('hid', 'seq'), may hold values from -0.125 to 0.125
- gate_rows: int32 [4, 448], P('hid'), may hold values from 0 to 31, as said below
- gate_cols: int32 [4, 448], P('hid'), may hold values from 0 to 27
- gate_count: int32 [4], P('hid'), may hold values from 56 to 448, as said below
- up_rows: int32 [4, 448], P('hid'), may hold values from 0 to 31, as said below
- up_cols: int32 [4, 448], P('hid'), may hold values from 0 to 27
- up_count: int32 [4], P('hid'), may hold values from 56 to 448, as said below
Outputs:
- hidden: bfloat16 [1024, 14336], P('seq', 'hid')
- input_grad: bfloat16 [1024, 4096], P('seq', 'hid')
- gate_block_grads: bfloat16 [4, 448, 128, 128], P('hid', 'seq')
- up_block_grads: bfloat16 [4, 448, 128, 128], P('hid', 'seq')
Inputs may be any that keep to these rules, and one draw needn't show every extreme that they name: For each panel, the pairs (gate_rows, gate_cols) over all 448 slots are distinct. `gate_count`: slots at or after a panel's count hold no block of the matrix. For each panel, the pairs (up_rows, up_cols) over all 448 slots are distinct. `up_count`: slots at or after a panel's count hold no block of the matrix.
All inputs are finite; a program needn't handle non-finite values.
Results may differ from a plain program's by a relative error of at most 0.018.
Values may be sent and summed in bfloat16 or wider, within the bound.
A program may use at most 192 MiB of HBM per device.

v0:
```python
import math
import jax
import jax.numpy as jnp
from jax import lax
from jax.sharding import PartitionSpec as P


def swapped(value, axis, stride):
    mask = 2**stride
    pairs = [(source, source ^ mask) for source in range(lax.axis_size(axis))]
    return lax.ppermute(value, axis, pairs)


def silu_parts(preact):
    sigma = jax.nn.sigmoid(preact)
    return (preact * sigma, sigma * (1.0 + preact * (1.0 - sigma)))


def place_split(products, placing, form):
    high_part = products.astype(jnp.bfloat16)
    rest_part = (products - high_part.astype(jnp.float32)).astype(jnp.bfloat16)
    table = placing.astype(jnp.bfloat16)
    placed = jnp.einsum(form, high_part, table, preferred_element_type=jnp.float32)
    return placed + jnp.einsum(form, rest_part, table, preferred_element_type=jnp.float32)


def project_slots(tiles, weights, rows, columns, live_count, group_size, trips, col_blocks):
    tok_rows = tiles.shape[0]
    block_size = tiles.shape[2]
    targets = jnp.arange(col_blocks)
    offsets = jnp.arange(group_size)

    def project_one_group(group_index, running):
        start = group_index * group_size
        chosen = lax.dynamic_slice_in_dim(weights, start, group_size, 0)
        row_ids = lax.dynamic_slice_in_dim(rows, start, group_size, 0)
        col_ids = lax.dynamic_slice_in_dim(columns, start, group_size, 0)
        active = start + offsets < live_count
        picked = jnp.take(tiles, row_ids, axis=1)
        products = jnp.einsum("tsk,skn->tsn", picked, chosen, preferred_element_type=jnp.float32)
        placing = (col_ids[:, None] == targets[None, :]) & active[:, None]
        return running + place_split(products, placing, "tsn,sc->tcn")

    initial = jnp.zeros((tok_rows, col_blocks, block_size), jnp.float32)
    return lax.fori_loop(0, trips, project_one_group, initial)


def return_slots(grad_tiles, weights, rows, columns, live_count, group_size, trips, row_blocks):
    tok_rows = grad_tiles.shape[0]
    block_size = grad_tiles.shape[2]
    targets = jnp.arange(row_blocks)
    offsets = jnp.arange(group_size)

    def return_one_group(group_index, running):
        start = group_index * group_size
        chosen = lax.dynamic_slice_in_dim(weights, start, group_size, 0)
        row_ids = lax.dynamic_slice_in_dim(rows, start, group_size, 0)
        col_ids = lax.dynamic_slice_in_dim(columns, start, group_size, 0)
        active = start + offsets < live_count
        picked = jnp.take(grad_tiles, col_ids, axis=1)
        products = jnp.einsum("tsn,skn->tsk", picked, chosen, preferred_element_type=jnp.float32)
        placing = (row_ids[:, None] == targets[None, :]) & active[:, None]
        return running + place_split(products, placing, "tsk,sr->trk")

    initial = jnp.zeros((tok_rows, row_blocks, block_size), jnp.float32)
    return lax.fori_loop(0, trips, return_one_group, initial)


def on_device(
    tokens,
    hidden_grad,
    gate_blocks,
    up_blocks,
    gate_rows,
    gate_cols,
    gate_count,
    up_rows,
    up_cols,
    up_count,
):
    gathered = lax.all_gather(tokens, "hid", axis=1, tiled=True)
    tok_rows = gathered.shape[0]
    block_size = gate_blocks.shape[2]
    row_blocks = gathered.shape[1] // block_size
    col_blocks = hidden_grad.shape[1] // block_size
    gate_all = lax.all_gather(gate_blocks, "seq", axis=1, tiled=True)
    up_all = lax.all_gather(up_blocks, "seq", axis=1, tiled=True)
    capacity = gate_all.shape[1]
    group_size = 32
    groups = capacity // group_size
    gate_live = gate_count[0]
    up_live = up_count[0]
    tiles = gathered.reshape(tok_rows, row_blocks, block_size)
    gate_pre = project_slots(
        tiles, gate_all[0], gate_rows[0], gate_cols[0], gate_live, group_size, groups, col_blocks
    )
    up_pre = project_slots(
        tiles, up_all[0], up_rows[0], up_cols[0], up_live, group_size, groups, col_blocks
    )
    activated, slope = silu_parts(gate_pre)
    hidden = (activated * up_pre).astype(jnp.bfloat16)
    upstream = hidden_grad.reshape(tok_rows, col_blocks, block_size).astype(jnp.float32)
    gate_grad = (upstream * up_pre * slope).astype(jnp.bfloat16)
    up_grad = (upstream * activated).astype(jnp.bfloat16)
    input_sum = return_slots(
        gate_grad,
        gate_all[0],
        gate_rows[0],
        gate_cols[0],
        gate_live,
        group_size,
        groups,
        row_blocks,
    )
    input_sum = input_sum + return_slots(
        up_grad, up_all[0], up_rows[0], up_cols[0], up_live, group_size, groups, row_blocks
    )
    input_grad = lax.psum_scatter(
        input_sum.reshape(tok_rows, row_blocks * block_size).astype(jnp.bfloat16),
        "hid",
        scatter_dimension=1,
        tiled=True,
    )
    seq_count = lax.axis_size("seq")
    position = lax.axis_index("seq")
    levels = seq_count.bit_length() - 1
    blk_dev = capacity // seq_count
    other_tiles, other_gate, other_up = swapped((tiles, gate_grad, up_grad), "seq", 0)
    both_tiles = jnp.concatenate([tiles, other_tiles], axis=0)
    both_gate = jnp.concatenate([gate_grad, other_gate], axis=0)
    both_up = jnp.concatenate([up_grad, other_up], axis=0)
    parity = position % 2
    owners = 2 * jnp.arange(seq_count // 2) + parity
    slot_ids = (owners[:, None] * blk_dev + jnp.arange(blk_dev)[None, :]).reshape(-1)
    stacked = []
    for rows, columns, live_count, grad_tiles in (
        (gate_rows[0], gate_cols[0], gate_live, both_gate),
        (up_rows[0], up_cols[0], up_live, both_up),
    ):
        row_ids = jnp.take(rows, slot_ids)
        col_ids = jnp.take(columns, slot_ids)
        picked_input = jnp.take(both_tiles, row_ids, axis=1)
        picked_grad = jnp.take(grad_tiles, col_ids, axis=1)
        block_term = jnp.einsum(
            "tsk,tsn->skn", picked_input, picked_grad, preferred_element_type=jnp.float32
        )
        stacked.append(block_term * (slot_ids < live_count).astype(jnp.float32)[:, None, None])
    current = jnp.stack(stacked, axis=1)
    current = current.reshape((seq_count // 2, blk_dev) + current.shape[1:])
    for level in range(1, levels):
        own_bit = position // 2**level % 2
        halves = current.reshape((current.shape[0] // 2, 2) + current.shape[1:])
        kept = lax.dynamic_index_in_dim(halves, own_bit, 1, keepdims=False)
        sent = lax.dynamic_index_in_dim(halves, 1 - own_bit, 1, keepdims=False)
        received = swapped(sent.astype(jnp.bfloat16), "seq", level)
        current = kept + received.astype(jnp.float32)
    summed = current[0]
    scale = 1.0 / math.sqrt(tok_rows * seq_count)
    gate_block_grads = (summed[:, 0] * scale).astype(jnp.bfloat16)[None]
    up_block_grads = (summed[:, 1] * scale).astype(jnp.bfloat16)[None]
    return (
        hidden.reshape(tok_rows, col_blocks * block_size),
        input_grad,
        gate_block_grads,
        up_block_grads,
    )


def solution(mesh):
    placed = (
        P("seq", "hid"),
        P("seq", "hid"),
        P("hid", "seq", None, None),
        P("hid", "seq", None, None),
        P("hid", None),
        P("hid", None),
        P("hid"),
        P("hid", None),
        P("hid", None),
        P("hid"),
    )
    return jax.shard_map(
        on_device,
        mesh=mesh,
        in_specs=placed,
        out_specs=(
            P("seq", "hid"),
            P("seq", "hid"),
            P("hid", "seq", None, None),
            P("hid", "seq", None, None),
        ),
        check_vma=False,
    )
```

profile of v0, /device:TPU:0, one launch (start us, length us, event | category | flops | bytes accessed | tf_op | source)
XLA Modules:
  0.0 1165.3 jit_solution(1844786483724718215)
XLA Ops:
  16.3 13.3 %all-gather.6.cloned.1.call-done = bf16[128,4096]{0,1:T(8,128)(2,1)} async-done(((bf16[128,1024]{0,1:T(8,128)(2,1)}), bf16[128,4096]{0,1:T(8,128)(2,1)}) %all-gather.6.cloned.1.call-update) | async-done | bytes 1048592 | tf_op jit(solution)/shard_map/all_gather | solution.py:81
  33.3 200.2 %all-gather.8.cloned.1.call-done = bf16[1,448,128,128]{3,2,0,1:T(8,128)(2,1)} async-done(((bf16[1,56,128,128]{3,2,0,1:T(8,128)(2,1)}), bf16[1,448,128,128]{3,2,0,1:T(8,128)(2,1)}) %all-gather.8.cloned.1.call-update) | async-done | bytes 14680080 | tf_op jit(solution)/shard_map/all_gather | solution.py:87
  233.5 192.3 %while.61 = (s32[]{:T(128)}, f32[128,28,128]{2,1,0:T(8,128)}, s32[448]{0:T(512)S(1)}, s32[]{:T(128)}, bf16[448,128,128]{2,1,0:T(8,128)(2,1)}, /*index=5*/s32[448...) while((s32[]{:T(128)}, f32[128,28,128]{2,1,0:T(8,128)}, ...), condition=%wide.region_3.5_spmd.clone, body=%wide.region_2.4_spmd.clone.sunk | while | flops 196940544 | bytes 19928416 | solution.py:45
  311.5 4.6 bitcast_add_fusion.9
  394.6 3.9 bitcast_add_fusion.9
  425.8 9.8 all-gather.4.cloned.1.call-done
  435.6 193.2 %while.60 = (s32[]{:T(128)}, f32[128,28,128]{2,1,0:T(8,128)}, s32[448]{0:T(512)S(1)}, s32[]{:T(128)}, bf16[448,128,128]{2,1,0:T(8,128)(2,1)}, /*index=5*/s32[448...) while((s32[]{:T(128)}, f32[128,28,128]{2,1,0:T(8,128)}, ...), condition=%wide.region_1.3_spmd.clone, body=%wide.region_0.2_spmd.clone.sunk | while | flops 196940544 | bytes 19928416 | solution.py:45
  569.6 3.8 bitcast_add_fusion.8
  628.8 6.5 multiply_convert_fusion.1
  645.1 9.4 gather_fusion.5
  654.5 9.2 gather_fusion.9
  665.3 9.2 gather_fusion.7
  678.0 9.1 gather_fusion.11
  687.2 18.4 %fusion.105 = f32[224,128,128]{2,1,0:T(8,128)} fusion(bf16[224,256,128]{2,1,0:T(8,128)(2,1)} %gather_fusion.7, pred[224]{0:T(512)(128)(4,1)S(1)} %get-tuple-element.961, bf16[224,256,128]{2,1,0:T(8,128)(2,1)} %gather_fusion.5, pred[224]{0:T(512)(128)(4,1)S(1)} %get-tuple-element.963, f32[224]{0:T(256)S(1)} %get-tuple-element.960), kind=kOutput, calls=%fused_computation.141 | convolution fusion | flops 1897398272 | bytes 44041536 | tf_op jit(solution)/shard_map/tsk,tsn->skn/dot_general | solution.py:144
  705.6 18.5 %fusion.110 = f32[224,128,128]{2,1,0:T(8,128)} fusion(bf16[224,256,128]{2,1,0:T(8,128)(2,1)} %gather_fusion.11, pred[224]{0:T(512)(128)(4,1)S(1)} %get-tuple-element.944, bf16[224,256,128]{2,1,0:T(8,128)(2,1)} %gather_fusion.9, pred[224]{0:T(512)(128)(4,1)S(1)} %get-tuple-element.941, f32[224]{0:T(256)S(1)} %get-tuple-element.959), kind=kOutput, calls=%fused_computation.142 | convolution fusion | flops 1897398272 | bytes 44041536 | tf_op jit(solution)/shard_map/tsk,tsn->skn/dot_general | solution.py:144
  724.1 10.1 fusion.115
  734.2 192.1 %while.62 = (s32[]{:T(128)}, f32[128,32,128]{2,1,0:T(8,128)}, s32[448]{0:T(512)S(1)}, s32[]{:T(128)}, bf16[448,128,128]{2,1,0:T(8,128)(2,1)}, /*index=5*/s32[448...) while((s32[]{:T(128)}, f32[128,32,128]{2,1,0:T(8,128)}, ...), condition=%wide.region_5.8_spmd.clone.clone, body=%wide.region_4.0_spmd.clone.clone.sunk | while | flops 205526272 | bytes 20976992 | solution.py:66
  757.1 3.9 bitcast_add_fusion.10
  770.9 3.9 bitcast_add_fusion.10
  784.7 3.9 bitcast_add_fusion.10
  798.5 3.9 bitcast_add_fusion.10
  812.2 3.9 bitcast_add_fusion.10
  826.0 3.9 bitcast_add_fusion.10
  839.8 3.9 bitcast_add_fusion.10
  853.5 3.9 bitcast_add_fusion.10
  867.3 3.9 bitcast_add_fusion.10
  881.1 3.9 bitcast_add_fusion.10
  894.8 3.9 bitcast_add_fusion.10
  908.6 3.9 bitcast_add_fusion.10
  922.4 3.9 bitcast_add_fusion.10
  926.2 8.6 fusion.90
  934.9 5.1 copy-done.7
  945.5 186.0 %while.63 = (s32[]{:T(128)}, f32[128,32,128]{2,1,0:T(8,128)}, s32[448]{0:T(512)}, s32[]{:T(128)}, bf16[448,128,128]{2,1,0:T(8,128)(2,1)}, /*index=5*/s32[448]{0:...) while((s32[]{:T(128)}, f32[128,32,128]{2,1,0:T(8,128)}, ...), condition=%wide.region_7.10_spmd.clone.clone, body=%wide.region_6.9_spmd.clone.clone.sunk | while | flops 205526272 | bytes 24647044 | solution.py:66
  967.5 3.9 bitcast_add_fusion.11
  980.9 3.9 bitcast_add_fusion.11
  994.2 3.9 bitcast_add_fusion.11
  1007.5 3.9 bitcast_add_fusion.11
  1020.9 3.9 bitcast_add_fusion.11
  1034.2 3.9 bitcast_add_fusion.11
  1047.5 3.9 bitcast_add_fusion.11
  1060.8 3.9 bitcast_add_fusion.11
  1074.2 3.9 bitcast_add_fusion.11
  1087.5 3.9 bitcast_add_fusion.11
  1100.8 3.9 bitcast_add_fusion.11
  1114.2 3.9 bitcast_add_fusion.11
  1127.5 3.9 bitcast_add_fusion.11
  1137.6 5.8 add_bitcast_fusion
  1146.2 12.6 %reduce-scatter.2.cloned.1.call-done = bf16[128,1024]{1,0:T(8,128)(2,1)} async-done(((bf16[128,4096]{1,0:T(8,128)(2,1)}), bf16[128,1024]{1,0:T(8,128)(2,1)}) %reduce-scatter.2.cloned.1.call-update) | async-done | bytes 262160 | tf_op jit(solution)/shard_map/reduce_scatter | solution.py:118
  (569 shorter events, 689.1 us)
Async XLA Ops:
  7.2 22.4 %all-gather.6.cloned.1.call-start = ((), (), s32[]{:S(2)}) async-start(), calls=%async_computation.2 | async-start | bytes 1310720 | tf_op jit(solution)/shard_map/all_gather | solution.py:81
  9.0 1.6 copy-start.9
  9.0 224.4 %all-gather.8.cloned.1.call-start = ((), (), s32[]{:S(2)}) async-start(), calls=%async_computation.3 | async-start | bytes 16515072 | tf_op jit(solution)/shard_map/all_gather | solution.py:87
  9.8 425.8 %all-gather.4.cloned.1.call-start = ((), (), s32[]{:S(2)}) async-start(), calls=%async_computation.1 | async-start | bytes 16515072 | tf_op jit(solution)/shard_map/all_gather | solution.py:86
  10.5 1148.3 %reduce-scatter.2.cloned.1.call-start = ((), (), s32[]{:S(2)}) async-start(), calls=%async_computation.4 | async-start | bytes 1310720 | tf_op jit(solution)/shard_map/reduce_scatter | solution.py:118
  10.6 3.7 copy-start.3
  12.8 220.6 %copy-start.2 = (s32[1,448]{1,0:T(1,128)S(1)}, s32[1,448]{1,0:T(1,128)}, u32[]{:S(2)}) copy-start(s32[1,448]{1,0:T(1,128)} %param.36) | copy-start | bytes 5380
  31.8 611.6 %collective-permute-start = (bf16[128,32,128]{2,0,1:T(8,128)(2,1)}, bf16[128,32,128]{2,0,1:T(8,128)(2,1)}, u32[]{:S(2)}, u32[]{:S(2)}) collective-permute-start(bf16[128,32,128]{2,0,1:T(8,128)(2,1)} %copy.98), channel_id=1, source_target_pairs={{0,4},{4,0},{8,12},{12,8},{16,20},{20,16},{24,28},{28,24},{1,5},{5... | collective-permute-start | bytes 3145736 | tf_op jit(solution)/shard_map/ppermute | solution.py:11
  233.5 202.1 %copy-start = (s32[1,448]{1,0:T(1,128)S(1)}, s32[1,448]{1,0:T(1,128)}, u32[]{:S(2)}) copy-start(s32[1,448]{1,0:T(1,128)} %param.33) | copy-start | bytes 5380
  233.5 202.1 %copy-start.1 = (s32[1,448]{1,0:T(1,128)S(1)}, s32[1,448]{1,0:T(1,128)}, u32[]{:S(2)}) copy-start(s32[1,448]{1,0:T(1,128)} %param.32) | copy-start | bytes 5380
  635.3 41.4 %copy-start.4 = (bf16[128,28,128]{2,0,1:T(8,128)(2,1)}, bf16[128,28,128]{2,0,1:T(8,128)(2,1)S(1)}, u32[]{:S(2)}) copy-start(bf16[128,28,128]{2,0,1:T(8,128)(2,1)S(1)} %get-tuple-element.1284) | copy-start | bytes 2752516
  635.3 28.4 %collective-permute-start.1 = (bf16[128,28,128]{2,0,1:T(8,128)(2,1)}, bf16[128,28,128]{2,0,1:T(8,128)(2,1)}, u32[]{:S(2)}, u32[]{:S(2)}) collective-permute-start(bf16[128,28,128]{2,0,1:T(8,128)(2,1)} %get-tuple-element.1251), channel_id=1, source_target_pairs={{0,4},{4,0},{8,12},{12,8},{16,20},{20,16},{24,28},{28,24},{1,5},{5... | collective-permute-start | bytes 2752520 | tf_op jit(solution)/shard_map/ppermute | solution.py:11
  635.9 40.8 %collective-permute-start.2 = (bf16[128,28,128]{2,0,1:T(8,128)(2,1)S(1)}, bf16[128,28,128]{2,0,1:T(8,128)(2,1)}, u32[]{:S(2)}, u32[]{:S(2)}) collective-permute-start(bf16[128,28,128]{2,0,1:T(8,128)(2,1)S(1)} %get-tuple-element.1284), channel_id=1, source_target_pairs={{0,4},{4,0},{8,12},{12,8},{16,20},{20,16},{24,28},{28,24},{1,5},{5... | collective-permute-start | bytes 2752520 | tf_op jit(solution)/shard_map/ppermute | solution.py:11
  734.2 192.1 %collective-permute-start.3 = (bf16[2,56,2,128,128]{4,3,1,2,0:T(8,128)(2,1)}, bf16[2,56,2,128,128]{4,3,1,2,0:T(8,128)(2,1)}, u32[]{:S(2)}, u32[]{:S(2)}) collective-permute-start(bf16[2,56,2,128,128]{4,3,1,2,0:T(8,128)(2,1)} %fusion.115), channel_id=1, source_target_pairs={{0,8},{4,12},{8,0},{12,4},{16,24},{20,28},{24,16},{28,20},{1,9},{5... | collective-permute-start | bytes 22020104 | tf_op jit(solution)/shard_map/ppermute | solution.py:11
  934.9 5.1 copy-start.7
  940.0 5.5 copy-start.5
  942.7 194.9 %collective-permute-start.4 = (bf16[1,56,2,128,128]{4,3,1,2,0:T(8,128)(2,1)}, bf16[1,56,2,128,128]{4,3,1,2,0:T(8,128)(2,1)}, u32[]{:S(2)}, u32[]{:S(2)}) collective-permute-start(bf16[1,56,2,128,128]{4,3,1,2,0:T(8,128)(2,1)} %dynamic-slice_convert_fusion), channel_id=1, source_target_pairs={{0,16},{4,20},{8,24},{12,28},{16,0},{20,4},{24,8},{28,12},{1,17},{... | collective-permute-start | bytes 11010056 | tf_op jit(solution)/shard_map/ppermute | solution.py:11
  954.9 3.3 copy-start.6
  967.5 3.9 copy-start.6
  980.9 3.9 copy-start.6
  994.2 3.9 copy-start.6
  1007.5 3.9 copy-start.6
  1020.9 3.9 copy-start.6
  1034.2 3.9 copy-start.6
  1047.5 3.9 copy-start.6
  1060.8 3.9 copy-start.6
  1074.2 3.9 copy-start.6
  1087.5 3.9 copy-start.6
  1100.8 3.9 copy-start.6
  1114.2 3.9 copy-start.6
  1127.5 3.9 copy-start.6
  1134.1 1.5 copy-start.8
Sparse Core Ops, SparseCore 0:
  10.1 19.4 all-gather.5
  31.8 201.6 all-gather.7
  235.7 199.8 all-gather.3
  1135.7 23.0 reduce-scatter.1
where the time goes:
time: 1170 us
  matrix products  462 us (39%)
  local copies, waits for them, and re-layouts  359 us (31%)
  waiting for transfers between devices  239 us (20%)
  other arithmetic  82.2 us (7%)
  between operations  15.4 us (1%)
    dot_general x56, matrix products, place_split(): jnp.einsum(form, rest_part, table, preferred_element_type=jnp.float32)  213 us
    all_gather x1, waiting for transfers between devices, on_device(): up_all = lax.all_gather(up_blocks, 'seq', axis=1, tiled=True)  200 us
    convert_element_type x56, local copies, waits for them, and re-layouts, place_split(): rest_part = (products - high_part.astype(jnp.float32)).astype(jnp.bfloat16)  95.1 us
    convert_element_type x56, local copies, waits for them, and re-layouts, place_split(): high_part = products.astype(jnp.bfloat16)  95 us
    dot_general x56, matrix products, place_split(): jnp.einsum(form, high_part, table, preferred_element_type=jnp.float32)  91.5 us
    dot_general x28, matrix products, return_one_group(): jnp.einsum('tsn,skn->tsk', picked, chosen, preferred_element_type=jnp.flo...  60.6 us
    dot_general x28, matrix products, project_one_group(): jnp.einsum('tsk,skn->tsn', picked, chosen, preferred_element_type=jnp.flo...  59.6 us
    gather x28, local copies, waits for them, and re-layouts, project_one_group(): picked = jnp.take(tiles, row_ids, axis=1)  55.3 us
  transfers between devices with their start and end apart: 9, of which 5 were waited for; matrix products, arithmetic and copies ran while one was open for 71% of the time, Pallas kernels for 0%

commit v1 on v0

--- a/solution.py
+++ b/solution.py
@@ -3,6 +3,12 @@
 import jax.numpy as jnp
 from jax import lax
 from jax.sharding import PartitionSpec as P
+
+
+def joined_along(tiles, dim):
+    dims = list(tiles.shape[1:])
+    dims[dim] *= tiles.shape[0]
+    return jnp.moveaxis(tiles, 0, dim).reshape(dims)
 
 
 def swapped(value, axis, stride):
@@ -84,7 +90,19 @@
     row_blocks = gathered.shape[1] // block_size
     col_blocks = hidden_grad.shape[1] // block_size
     gate_all = lax.all_gather(gate_blocks, "seq", axis=1, tiled=True)
-    up_all = lax.all_gather(up_blocks, "seq", axis=1, tiled=True)
+    size = lax.axis_size("seq")
+    pairs_2 = [(i, (i + 1) % size) for i in range(size)]
+    back = [(b, a) for a, b in pairs_2]
+    lower, upper = ([], [])
+    for turn in range(size - 1):
+        if turn % 2 == 0:
+            lower.append(lax.ppermute(lower[-1] if lower else up_blocks, "seq", pairs_2))
+        else:
+            upper.append(lax.ppermute(upper[-1] if upper else up_blocks, "seq", back))
+    pieces = jnp.stack([*lower[::-1], up_blocks, *upper])
+    shift = lax.axis_index("seq") - len(lower)
+    pieces = pieces[(jnp.arange(size) - shift) % size]
+    up_all = joined_along(pieces, 1)
     capacity = gate_all.shape[1]
     group_size = 32
     groups = capacity // group_size

time: 1170 us -> 1340 us (1.15)
  waiting for transfers between devices: 239 us -> 375 us
  starting transfers between devices: 6.42 us -> 29 us
  local copies, waits for them, and re-layouts: 359 us -> 376 us
    ppermute x0 -> x7, waiting for transfers between devices: none -> 362 us  [the longest x4 347 us: on_device(): lax.ppermute(lower[-1] if lower else up_blocks, 'seq', pairs_2)]
    all_gather x1 -> x0, waiting for transfers between devices: 200 us -> none  [on_device(): up_all = lax.all_gather(up_blocks, 'seq', axis=1, tiled=True)]
    ppermute x0 -> x7, starting transfers between devices: none -> 22.5 us  [the longest x3 13.8 us: on_device(): upper.append(lax.ppermute(upper[-1] if upper else up_blocks, 'seq', back))]
    unnamed x23 -> x36, local copies, waits for them, and re-layouts: 12.6 us -> 29.1 us
  transfers between devices with their start and end apart: 9 -> 15, of which waited for: 5 -> 9; matrix products, arithmetic and copies ran while one was open for 71% -> 62% of each run, Pallas kernels for 0% -> 0%
where the time goes in v1:
time: 1340 us; the launch traced here: 1330 us
  matrix products  453 us (34%)
  local copies, waits for them, and re-layouts  376 us (28%)
  waiting for transfers between devices  375 us (28%)
  other arithmetic  82.4 us (6%)
  starting transfers between devices  29 us (2%)
  between operations  15.6 us (1%)
    ppermute x4, waiting for transfers between devices, on_device(): lax.ppermute(lower[-1] if lower else up_blocks, 'seq', pairs_2)  347 us
    dot_general x56, matrix products, place_split(): jnp.einsum(form, rest_part, table, preferred_element_type=jnp.float32)  205 us
    convert_element_type x56, local copies, waits for them, and re-layouts, place_split(): rest_part = (products - high_part.astype(jnp.float32)).astype(jnp.bfloat16)  93.8 us
    convert_element_type x56, local copies, waits for them, and re-layouts, place_split(): high_part = products.astype(jnp.bfloat16)  93.8 us
    dot_general x56, matrix products, place_split(): jnp.einsum(form, high_part, table, preferred_element_type=jnp.float32)  91.5 us
    dot_general x28, matrix products, return_one_group(): jnp.einsum('tsn,skn->tsk', picked, chosen, preferred_element_type=jnp.flo...  60.3 us
    dot_general x28, matrix products, project_one_group(): jnp.einsum('tsk,skn->tsn', picked, chosen, preferred_element_type=jnp.flo...  59.5 us
    gather x28, local copies, waits for them, and re-layouts, project_one_group(): picked = jnp.take(tiles, row_ids, axis=1)  55.2 us
  transfers between devices with their start and end apart: 15, of which 9 were waited for; matrix products, arithmetic and copies ran while one was open for 62% of the time, Pallas kernels for 0%

profile of v1, /device:TPU:0, one launch (start us, length us, event | category | flops | bytes accessed | tf_op | source)
XLA Modules:
  0.0 1332.6 jit_solution(17125275692493648881)
XLA Ops:
  12.8 48.0 %collective-permute-done = bf16[1,56,128,128]{3,2,1,0:T(8,128)(2,1)S(1)} collective-permute-done((bf16[1,56,128,128]{3,2,1,0:T(8,128)(2,1)}, bf16[1,56,128,128]{3,2,1,0:T(8,128)(2,1)S(1)}, u32[]{:S(2)}, u32[]{:S(2)}) %collective-permute-start) | collective-permute-done | bytes 1835040 | tf_op jit(solution)/shard_map/ppermute | solution.py:99
  61.5 4.1 collective-permute-start.4
  65.6 82.4 %collective-permute-done.1 = bf16[1,56,128,128]{3,2,1,0:T(8,128)(2,1)S(1)} collective-permute-done((bf16[1,56,128,128]{3,2,1,0:T(8,128)(2,1)S(1)}, bf16[1,56,128,128]{3,2,1,0:T(8,128)(2,1)S(1)}, u32[]{:S(2)}, u32[]{:S(2)}) %collective-permute-start.1) | collective-permute-done | bytes 1835040 | tf_op jit(solution)/shard_map/ppermute | solution.py:99
  154.8 114.2 %collective-permute-done.2 = bf16[1,56,128,128]{3,2,1,0:T(8,128)(2,1)} collective-permute-done((bf16[1,56,128,128]{3,2,1,0:T(8,128)(2,1)S(1)}, bf16[1,56,128,128]{3,2,1,0:T(8,128)(2,1)}, u32[]{:S(2)}, u32[]{:S(2)}) %collective-permute-start.2) | collective-permute-done | bytes 1835040 | tf_op jit(solution)/shard_map/ppermute | solution.py:99
  279.1 6.8 collective-permute-start.6
  286.0 102.4 %collective-permute-done.3 = bf16[1,56,128,128]{3,2,1,0:T(8,128)(2,1)} collective-permute-done((bf16[1,56,128,128]{3,2,1,0:T(8,128)(2,1)}, bf16[1,56,128,128]{3,2,1,0:T(8,128)(2,1)}, u32[]{:S(2)}, u32[]{:S(2)}) %collective-permute-start.3) | collective-permute-done | bytes 1835040 | tf_op jit(solution)/shard_map/ppermute | solution.py:99
  397.5 14.6 %collective-permute-done.6 = bf16[1,56,128,128]{3,2,1,0:T(8,128)(2,1)S(1)} collective-permute-done((bf16[1,56,128,128]{3,2,1,0:T(8,128)(2,1)}, bf16[1,56,128,128]{3,2,1,0:T(8,128)(2,1)S(1)}, u32[]{:S(2)}, u32[]{:S(2)}) %collective-permute-start.6) | collective-permute-done | bytes 1835040 | tf_op jit(solution)/shard_map/ppermute | solution.py:101
  412.3 5.2 copy-done.8
  417.5 12.9 gather_fusion.4
  430.5 190.1 %while.61 = (s32[]{:T(128)}, f32[128,28,128]{2,1,0:T(8,128)}, s32[448]{0:T(512)S(1)}, s32[]{:T(128)}, bf16[448,128,128]{2,1,0:T(8,128)(2,1)}, /*index=5*/s32[448...) while((s32[]{:T(128)}, f32[128,28,128]{2,1,0:T(8,128)}, ...), condition=%wide.region_3.5_spmd.clone, body=%wide.region_2.4_spmd.clone.sunk | while | flops 196940544 | bytes 19928416 | solution.py:51
  453.4 3.7 bitcast_add_fusion.9
  467.0 3.7 bitcast_add_fusion.9
  480.6 3.7 bitcast_add_fusion.9
  494.3 3.7 bitcast_add_fusion.9
  507.9 3.7 bitcast_add_fusion.9
  521.5 3.7 bitcast_add_fusion.9
  535.1 3.7 bitcast_add_fusion.9
  548.8 3.7 bitcast_add_fusion.9
  562.4 3.7 bitcast_add_fusion.9
  620.6 189.9 %while.60 = (s32[]{:T(128)}, f32[128,28,128]{2,1,0:T(8,128)}, s32[448]{0:T(512)S(1)}, s32[]{:T(128)}, bf16[448,128,128]{2,1,0:T(8,128)(2,1)}, /*index=5*/s32[448...) while((s32[]{:T(128)}, f32[128,28,128]{2,1,0:T(8,128)}, ...), condition=%wide.region_1.3_spmd.clone, body=%wide.region_0.2_spmd.clone.sunk | while | flops 196940544 | bytes 19928416 | solution.py:51
  810.5 6.6 multiply_convert_fusion.1
  828.8 9.4 gather_fusion.6
  838.2 9.2 gather_fusion.10
  849.1 9.2 gather_fusion.8
  860.1 9.1 gather_fusion.12
  869.3 18.2 %fusion.105 = f32[224,128,128]{2,1,0:T(8,128)} fusion(bf16[224,256,128]{2,1,0:T(8,128)(2,1)} %gather_fusion.8, pred[224]{0:T(512)(128)(4,1)S(1)} %get-tuple-element.961, bf16[224,256,128]{2,1,0:T(8,128)(2,1)} %gather_fusion.6, pred[224]{0:T(512)(128)(4,1)S(1)} %get-tuple-element.963, f32[224]{0:T(256)S(1)} %get-tuple-element.960), kind=kOutput, calls=%fused_computation.142 | convolution fusion | flops 1897398272 | bytes 44041536 | tf_op jit(solution)/shard_map/tsk,tsn->skn/dot_general | solution.py:162
  887.5 18.4 %fusion.110 = f32[224,128,128]{2,1,0:T(8,128)} fusion(bf16[224,256,128]{2,1,0:T(8,128)(2,1)} %gather_fusion.12, pred[224]{0:T(512)(128)(4,1)S(1)} %get-tuple-element.944, bf16[224,256,128]{2,1,0:T(8,128)(2,1)} %gather_fusion.10, pred[224]{0:T(512)(128)(4,1)S(1)} %get-tuple-element.941, f32[224]{0:T(256)S(1)} %get-tuple-element.959), kind=kOutput, calls=%fused_computation.143 | convolution fusion | flops 1897398272 | bytes 44041536 | tf_op jit(solution)/shard_map/tsk,tsn->skn/dot_general | solution.py:162
  906.0 10.1 fusion.115
  916.1 189.2 %while.62 = (s32[]{:T(128)}, f32[128,32,128]{2,1,0:T(8,128)}, s32[448]{0:T(512)S(1)}, s32[]{:T(128)}, bf16[448,128,128]{2,1,0:T(8,128)(2,1)}, /*index=5*/s32[448...) while((s32[]{:T(128)}, f32[128,32,128]{2,1,0:T(8,128)}, ...), condition=%wide.region_5.8_spmd.clone.clone, body=%wide.region_4.7_spmd.clone.clone.sunk | while | flops 205526272 | bytes 20976992 | solution.py:72
  1105.3 8.6 fusion.90
  1113.9 5.2 copy-done.7
  1121.8 3.8 collective-permute-start.11
  1125.6 173.6 %while.63 = (s32[]{:T(128)}, f32[128,32,128]{2,1,0:T(8,128)}, s32[448]{0:T(512)S(1)}, s32[]{:T(128)}, bf16[448,128,128]{2,1,0:T(8,128)(2,1)}, /*index=5*/s32[448...) while((s32[]{:T(128)}, f32[128,32,128]{2,1,0:T(8,128)}, ...), condition=%wide.region_7.10_spmd.clone.clone, body=%wide.region_6.9_spmd.clone.clone.sunk | while | flops 205526272 | bytes 24647044 | solution.py:72
  1146.1 3.7 bitcast_add_fusion.11
  1158.6 3.7 bitcast_add_fusion.11
  1171.0 3.7 bitcast_add_fusion.11
  1183.5 3.7 bitcast_add_fusion.11
  1195.9 3.7 bitcast_add_fusion.11
  1208.4 3.7 bitcast_add_fusion.11
  1220.8 3.7 bitcast_add_fusion.11
  1233.2 3.7 bitcast_add_fusion.11
  1245.7 3.7 bitcast_add_fusion.11
  1258.1 3.7 bitcast_add_fusion.11
  1270.6 3.7 bitcast_add_fusion.11
  1283.0 3.7 bitcast_add_fusion.11
  1295.5 3.7 bitcast_add_fusion.11
  1305.4 5.9 add_bitcast_fusion
  1314.1 11.7 reduce-scatter.2.cloned.1.call-done
  (596 shorter events, 717.3 us)
Async XLA Ops:
  7.2 269.0 %all-gather.5.cloned.1.call-start = ((), (), s32[]{:S(2)}) async-start(), calls=%async_computation.2 | async-start | bytes 1310720 | tf_op jit(solution)/shard_map/all_gather | solution.py:87
  7.2 53.6 %collective-permute-start = (bf16[1,56,128,128]{3,2,1,0:T(8,128)(2,1)}, bf16[1,56,128,128]{3,2,1,0:T(8,128)(2,1)S(1)}, u32[]{:S(2)}, u32[]{:S(2)}) collective-permute-start(bf16[1,56,128,128]{3,2,1,0:T(8,128)(2,1)} %param.31), channel_id=1, source_target_pairs={{0,4},{4,8},{8,12},{12,16},{16,20},{20,24},{24,28},{28,0},{1,5},{5... | collective-permute-start | bytes 5505032 | tf_op jit(solution)/shard_map/ppermute | solution.py:99
  12.0 608.6 %all-gather.3.cloned.1.call-start = ((), (), s32[]{:S(2)}) async-start(), calls=%async_computation.1 | async-start | bytes 16515072 | tf_op jit(solution)/shard_map/all_gather | solution.py:92
  12.8 1313.0 %reduce-scatter.2.cloned.1.call-start = ((), (), s32[]{:S(2)}) async-start(), calls=%async_computation.3 | async-start | bytes 1310720 | tf_op jit(solution)/shard_map/reduce_scatter | solution.py:136
  60.8 87.2 %collective-permute-start.1 = (bf16[1,56,128,128]{3,2,1,0:T(8,128)(2,1)S(1)}, bf16[1,56,128,128]{3,2,1,0:T(8,128)(2,1)S(1)}, u32[]{:S(2)}, u32[]{:S(2)}) collective-permute-start(bf16[1,56,128,128]{3,2,1,0:T(8,128)(2,1)S(1)} %collective-permute-done), channel_id=1, source_target_pairs={{0,4},{4,8},{8,12},{12,16},{16,20},{20,24},{24,28},{28,0},{1,5},{5... | collective-permute-start | bytes 5505032 | tf_op jit(solution)/shard_map/ppermute | solution.py:99
  61.5 90.4 %collective-permute-start.4 = (bf16[1,56,128,128]{3,2,1,0:T(8,128)(2,1)}, bf16[1,56,128,128]{3,2,1,0:T(8,128)(2,1)}, u32[]{:S(2)}, u32[]{:S(2)}) collective-permute-start(bf16[1,56,128,128]{3,2,1,0:T(8,128)(2,1)} %param.31), channel_id=1, source_target_pairs={{4,0},{8,4},{12,8},{16,12},{20,16},{24,20},{28,24},{0,28},{5,1},{9... | collective-permute-start | bytes 5505032 | tf_op jit(solution)/shard_map/ppermute | solution.py:101
  148.0 1.2 copy-start.11
  149.2 119.7 %collective-permute-start.2 = (bf16[1,56,128,128]{3,2,1,0:T(8,128)(2,1)S(1)}, bf16[1,56,128,128]{3,2,1,0:T(8,128)(2,1)}, u32[]{:S(2)}, u32[]{:S(2)}) collective-permute-start(bf16[1,56,128,128]{3,2,1,0:T(8,128)(2,1)S(1)} %collective-permute-done.1), channel_id=1, source_target_pairs={{0,4},{4,8},{8,12},{12,16},{16,20},{20,24},{24,28},{28,0},{1,5},{5... | collective-permute-start | bytes 5505032 | tf_op jit(solution)/shard_map/ppermute | solution.py:99
  151.9 127.2 %collective-permute-start.5 = (bf16[1,56,128,128]{3,2,1,0:T(8,128)(2,1)}, bf16[1,56,128,128]{3,2,1,0:T(8,128)(2,1)}, u32[]{:S(2)}, u32[]{:S(2)}) collective-permute-start(bf16[1,56,128,128]{3,2,1,0:T(8,128)(2,1)} %collective-permute-done.4), channel_id=1, source_target_pairs={{4,0},{8,4},{12,8},{16,12},{20,16},{24,20},{28,24},{0,28},{5,1},{9... | collective-permute-start | bytes 5505032 | tf_op jit(solution)/shard_map/ppermute | solution.py:101
  269.0 119.4 %collective-permute-start.3 = (bf16[1,56,128,128]{3,2,1,0:T(8,128)(2,1)}, bf16[1,56,128,128]{3,2,1,0:T(8,128)(2,1)}, u32[]{:S(2)}, u32[]{:S(2)}) collective-permute-start(bf16[1,56,128,128]{3,2,1,0:T(8,128)(2,1)} %collective-permute-done.2), channel_id=1, source_target_pairs={{0,4},{4,8},{8,12},{12,16},{16,20},{20,24},{24,28},{28,0},{1,5},{5... | collective-permute-start | bytes 5505032 | tf_op jit(solution)/shard_map/ppermute | solution.py:99
  278.5 113.5 %copy-start.12 = (bf16[1,56,128,128]{3,2,1,0:T(8,128)(2,1)S(1)}, bf16[1,56,128,128]{3,2,1,0:T(8,128)(2,1)}, u32[]{:S(2)}) copy-start(bf16[1,56,128,128]{3,2,1,0:T(8,128)(2,1)} %copy-done.11) | copy-start | bytes 5505028
  278.5 548.6 %collective-permute-start.7 = (bf16[128,32,128]{2,0,1:T(8,128)(2,1)}, bf16[128,32,128]{2,0,1:T(8,128)(2,1)}, u32[]{:S(2)}, u32[]{:S(2)}) collective-permute-start(bf16[128,32,128]{2,0,1:T(8,128)(2,1)} %copy.98), channel_id=1, source_target_pairs={{0,4},{4,0},{8,12},{12,8},{16,20},{20,16},{24,28},{28,24},{1,5},{5... | collective-permute-start | bytes 3145736 | tf_op jit(solution)/shard_map/ppermute | solution.py:17
  279.1 132.9 %collective-permute-start.6 = (bf16[1,56,128,128]{3,2,1,0:T(8,128)(2,1)}, bf16[1,56,128,128]{3,2,1,0:T(8,128)(2,1)S(1)}, u32[]{:S(2)}, u32[]{:S(2)}) collective-permute-start(bf16[1,56,128,128]{3,2,1,0:T(8,128)(2,1)} %collective-permute-done.5), channel_id=1, source_target_pairs={{4,0},{8,4},{12,8},{16,12},{20,16},{24,20},{28,24},{0,28},{5,1},{9... | collective-permute-start | bytes 5505032 | tf_op jit(solution)/shard_map/ppermute | solution.py:101
  392.0 1.6 copy-start.10
  412.3 5.2 copy-start.8
  417.5 12.9 copy-start.2
  417.5 12.9 copy-start.3
  430.5 190.1 %copy-start = (s32[1,448]{1,0:T(1,128)S(1)}, s32[1,448]{1,0:T(1,128)}, u32[]{:S(2)}) copy-start(s32[1,448]{1,0:T(1,128)} %param.33) | copy-start | bytes 5380
  430.5 190.1 %copy-start.1 = (s32[1,448]{1,0:T(1,128)S(1)}, s32[1,448]{1,0:T(1,128)}, u32[]{:S(2)}) copy-start(s32[1,448]{1,0:T(1,128)} %param.32) | copy-start | bytes 5380
  817.1 41.7 %copy-start.4 = (bf16[128,28,128]{2,0,1:T(8,128)(2,1)}, bf16[128,28,128]{2,0,1:T(8,128)(2,1)S(1)}, u32[]{:S(2)}) copy-start(bf16[128,28,128]{2,0,1:T(8,128)(2,1)S(1)} %get-tuple-element.1286) | copy-start | bytes 2752516
  817.1 30.4 %collective-permute-start.8 = (bf16[128,28,128]{2,0,1:T(8,128)(2,1)}, bf16[128,28,128]{2,0,1:T(8,128)(2,1)}, u32[]{:S(2)}, u32[]{:S(2)}) collective-permute-start(bf16[128,28,128]{2,0,1:T(8,128)(2,1)} %get-tuple-element.1253), channel_id=1, source_target_pairs={{0,4},{4,0},{8,12},{12,8},{16,20},{20,16},{24,28},{28,24},{1,5},{5... | collective-permute-start | bytes 2752520 | tf_op jit(solution)/shard_map/ppermute | solution.py:17
  825.0 33.8 %collective-permute-start.9 = (bf16[128,28,128]{2,0,1:T(8,128)(2,1)S(1)}, bf16[128,28,128]{2,0,1:T(8,128)(2,1)}, u32[]{:S(2)}, u32[]{:S(2)}) collective-permute-start(bf16[128,28,128]{2,0,1:T(8,128)(2,1)S(1)} %get-tuple-element.1286), channel_id=1, source_target_pairs={{0,4},{4,0},{8,12},{12,8},{16,20},{20,16},{24,28},{28,24},{1,5},{5... | collective-permute-start | bytes 2752520 | tf_op jit(solution)/shard_map/ppermute | solution.py:17
  916.1 189.2 %collective-permute-start.10 = (bf16[2,56,2,128,128]{4,3,1,2,0:T(8,128)(2,1)}, bf16[2,56,2,128,128]{4,3,1,2,0:T(8,128)(2,1)}, u32[]{:S(2)}, u32[]{:S(2)}) collective-permute-start(bf16[2,56,2,128,128]{4,3,1,2,0:T(8,128)(2,1)} %fusion.115), channel_id=1, source_target_pairs={{0,8},{4,12},{8,0},{12,4},{16,24},{20,28},{24,16},{28,20},{1,9},{5... | collective-permute-start | bytes 22020104 | tf_op jit(solution)/shard_map/ppermute | solution.py:17
  1113.9 5.2 copy-start.7
  1119.1 6.5 copy-start.5
  1121.8 183.6 %collective-permute-start.11 = (bf16[1,56,2,128,128]{4,3,1,2,0:T(8,128)(2,1)}, bf16[1,56,2,128,128]{4,3,1,2,0:T(8,128)(2,1)}, u32[]{:S(2)}, u32[]{:S(2)}) collective-permute-start(bf16[1,56,2,128,128]{4,3,1,2,0:T(8,128)(2,1)} %dynamic-slice_convert_fusion), channel_id=1, source_target_pairs={{0,16},{4,20},{8,24},{12,28},{16,0},{20,4},{24,8},{28,12},{1,17},{... | collective-permute-start | bytes 11010056 | tf_op jit(solution)/shard_map/ppermute | solution.py:17
  1134.3 3.1 copy-start.6
  1146.1 3.7 copy-start.6
  1158.6 3.7 copy-start.6
  1171.0 3.7 copy-start.6
  1183.5 3.7 copy-start.6
  1195.9 3.7 copy-start.6
  1208.3 3.7 copy-start.6
  1220.8 3.7 copy-start.6
  1233.2 3.7 copy-start.6
  1245.7 3.7 copy-start.6
  1258.1 3.7 copy-start.6
  1270.6 3.7 copy-start.6
  1283.0 3.7 copy-start.6
  1295.5 3.7 copy-start.6
  1299.2 4.3 copy-start.9
Sparse Core Ops, SparseCore 0:
  12.2 17.3 all-gather.4
  31.8 401.0 all-gather.2
  1303.6 22.1 reduce-scatter.1
